TPU v7x, 32 devices: a whole 2x2x4 slice. The times are simulated.
32 devices in a mesh: seq: 16 (over z, y, core), dp: 2 (over x).
Axes of the slice: x: 2, y: 2, z: 4, core: 2. Of those that a mesh axis runs over, the one named last changes fastest.
Arguments:
- layer_input: bfloat16 [2, 2048, 4096], P('dp', 'seq'), may hold values from -0.3125 to 0.3125
- scan_input: bfloat16 [2, 2048, 2048], P('dp', 'seq'), may hold values from -6 to 6
- readout: bfloat16 [2, 2048, 64], P('dp', 'seq'), may hold values from -6 to 6
- log_decay: float32 [2, 2048, 32], P('dp', 'seq'), may hold values from -1 to 0
- output_cotangent: bfloat16 [2, 2048, 2048], P('dp', 'seq'), may hold values from -0.0078125 to 0.0078125
- write_weight: float32 [4096, 64], P('dp'), may hold values from -6 to 6
- first_moment: float32 [4096, 64], P('dp'), may hold values from -6 to 6
- second_moment: float32 [4096, 64], P('dp'), may hold values from 1 to 25
Outputs:
- decay_gradient: float32 [2, 2048, 32], P('dp', 'seq')
- new_weight: float32 [4096, 64], P('dp')
- new_first: float32 [4096, 64], P('dp')
- new_second: float32 [4096, 64], P('dp')
All inputs are finite; a program needn't handle non-finite values.
Results may differ from a plain program's by a relative error of at most 0.0039.
Values may be sent and summed in bfloat16 or wider, within the bound.
A program may use at most 64 MiB of HBM per device.

v0:
```python
import jax
import jax.numpy as jnp
from jax import lax
from jax.sharding import PartitionSpec as P

HALF_HEAD_COUNT = 32
HEAD_DIM = 64
STATE = 64


beta_one = 0.9
beta_two = 0.999
adam_count = 10.0
learn_rate = 0.01
weight_decay = 0.1
epsilon = 1e-08
highest = lax.Precision.HIGHEST


def entering(part, axis, combine, identity, reverse):
    count = lax.axis_size(axis)
    place = lax.axis_index(axis)
    ahead = count - 1 - place if reverse else place
    gathered = jax.tree.map(lambda a: lax.all_gather(a, axis), part)
    state = jax.tree.map(lambda a, e: jnp.zeros_like(a) + jnp.asarray(e, a.dtype), part, identity)

    def one(lap, state):
        source = count - 1 - lap if reverse else lap
        return combine(
            state, jax.tree.map(lambda a: lax.dynamic_index_in_dim(a, source, 0, False), gathered)
        )

    return lax.fori_loop(0, ahead, one, state)


def pair_combine(earlier_pair, later_pair):
    return (
        earlier_pair[0] * later_pair[0],
        later_pair[0][:, None, None] * earlier_pair[1] + later_pair[1],
    )


def adam_update(grad_rows, weight_rows, first_rows, second_rows):
    new_first = beta_one * first_rows + (1.0 - beta_one) * grad_rows
    new_second = beta_two * second_rows + (1.0 - beta_two) * grad_rows * grad_rows
    first_hat = new_first / (1.0 - beta_one**adam_count)
    second_hat = new_second / (1.0 - beta_two**adam_count)
    new_weight = weight_rows - learn_rate * (
        first_hat / (jnp.sqrt(second_hat) + epsilon) + weight_decay * weight_rows
    )
    return (new_weight, new_first, new_second)


def on_device(
    layer_input,
    scan_input,
    readout,
    log_decay,
    output_cotangent,
    write_weight,
    first_moment,
    second_moment,
):
    input_rows = layer_input[0]
    scan_rows = scan_input[0]
    read_rows = readout[0]
    decay_rows = log_decay[0]
    back_rows = output_cotangent[0]
    length = input_rows.shape[0]
    weight_half = write_weight.astype(jnp.bfloat16)
    write_sum = jnp.dot(
        input_rows,
        lax.all_gather(weight_half, "dp", axis=0, tiled=True),
        preferred_element_type=jnp.float32,
    )
    write_half = write_sum.astype(jnp.bfloat16)
    write_float = lax.optimization_barrier(write_half).astype(jnp.float32)
    running = jnp.cumsum(decay_rows, axis=0)
    overall = running[-1]
    to_end = jnp.exp(overall[None, :] - running)
    from_start = jnp.exp(running)
    scan_split = scan_rows.reshape(length, HALF_HEAD_COUNT, HEAD_DIM)
    back_split = back_rows.reshape(length, HALF_HEAD_COUNT, HEAD_DIM)
    scan_heads = scan_split.astype(jnp.float32)
    back_heads = back_split.astype(jnp.float32)
    read_float = read_rows.astype(jnp.float32)
    state_local = jnp.einsum(
        "shp,sn->hpn", scan_heads * to_end[:, :, None], write_float, precision=highest
    )
    reverse_local = jnp.einsum(
        "shp,sn->hpn", back_heads * from_start[:, :, None], read_float, precision=highest
    )
    decay_total = jnp.exp(overall)
    identity = (
        jnp.ones((HALF_HEAD_COUNT,), jnp.float32),
        jnp.zeros((HALF_HEAD_COUNT, HEAD_DIM, STATE), jnp.float32),
    )
    state_pair = entering((decay_total, state_local), "seq", pair_combine, identity, False)
    grad_pair = entering((decay_total, reverse_local), "seq", pair_combine, identity, True)
    state_before = state_pair[1]
    grad_after = grad_pair[1]
    term_one = decay_total * jnp.sum(grad_after * state_before, axis=(1, 2))
    grad_write = jnp.einsum("hpn,sn->shp", grad_after, write_float, precision=highest)
    second_rows = to_end * jnp.sum(scan_heads * grad_write, axis=2)
    term_two = jnp.cumsum(second_rows, axis=0) - second_rows
    state_read = jnp.einsum("hpn,sn->shp", state_before, read_float, precision=highest)
    third_rows = from_start * jnp.sum(back_heads * state_read, axis=2)
    term_three = jnp.flip(jnp.cumsum(jnp.flip(third_rows, 0), axis=0), 0)
    crossed = jnp.einsum("thp,shp->hts", scan_split, back_split, preferred_element_type=jnp.float32)
    heads_running = running.T
    spread = heads_running[:, None, :] - heads_running[:, :, None]
    row_index = lax.broadcasted_iota(jnp.int32, (length, length), 0)
    col_index = lax.broadcasted_iota(jnp.int32, (length, length), 1)
    kernel_mat = (
        jnp.where((row_index <= col_index)[None], jnp.exp(jnp.minimum(spread, 0.0)), 0.0) * crossed
    )
    write_read = jnp.dot(write_half, read_rows.T, preferred_element_type=jnp.float32)
    pairing = jnp.where((row_index < col_index)[None], kernel_mat * write_read[None], 0.0)
    balance = (jnp.sum(pairing, axis=2) - jnp.sum(pairing, axis=1)).T
    term_four = jnp.cumsum(balance, axis=0) - balance
    decay_grad = term_one[None, :] + term_two + term_three + term_four
    scaled_scan = (scan_heads * to_end[:, :, None]).reshape(length, HALF_HEAD_COUNT * HEAD_DIM)
    write_grad = jnp.dot(
        scaled_scan, grad_after.reshape(HALF_HEAD_COUNT * HEAD_DIM, STATE), precision=highest
    )
    write_grad = write_grad + jnp.dot(jnp.sum(kernel_mat, axis=0), read_float, precision=highest)
    grad_half = write_grad.astype(jnp.bfloat16)
    partial_grad = jnp.dot(input_rows.T, grad_half, preferred_element_type=jnp.float32)
    owner_grad = lax.psum_scatter(partial_grad, "dp", scatter_dimension=0, tiled=True)
    grad_rows = lax.psum(owner_grad, "seq")
    new_weight, new_first, new_second = adam_update(
        grad_rows, write_weight, first_moment, second_moment
    )
    return (decay_grad[None], new_weight, new_first, new_second)


def solution(mesh):
    in_specs = (
        P("dp", "seq", None),
        P("dp", "seq", None),
        P("dp", "seq", None),
        P("dp", "seq", None),
        P("dp", "seq", None),
        P("dp", None),
        P("dp", None),
        P("dp", None),
    )
    out_specs = (P("dp", "seq", None), P("dp", None), P("dp", None), P("dp", None))
    return jax.shard_map(
        on_device, mesh=mesh, in_specs=in_specs, out_specs=out_specs, check_vma=False
    )
```

profile of v0, /device:TPU:29, one launch (start us, length us, event | category | flops | bytes accessed | tf_op | source)
XLA Modules:
  0.0 436.1 jit_solution(12412782208266294412)
XLA Ops:
  9.8 1.6 fusion.17
  11.9 7.8 %all_gather.24 = bf16[4096,64]{0,1:T(8,128)(2,1)S(1)} all-gather(bf16[2048,64]{0,1:T(8,128)(2,1)S(1)} %convert_element_type.22), channel_id=1, replica_groups=mesh['seq'=16,'dp'=2] {'dp'}, dimensions={0}, use_global_device_ids=true | all-gather | bytes 786432 | tf_op jit(solution)/shard_map/all_gather | solution.py:73
  20.3 18.4 %all-gather.2 = f32[16,1,32]{2,1,0:T(1,128)S(1)} all-gather(f32[1,1,32]{2,1,0:T(1,128)S(1)} %get-tuple-element.175), channel_id=1, replica_groups=mesh['seq'=16,'dp'=2] {'seq'}, dimensions={0}, use_global_device_ids=true | all-gather | bytes 2176 | tf_op jit(solution)/shard_map/all_gather | solution.py:24
  38.9 1.8 fusion
  40.8 95.8 %all-gather.6.cloned.1.call-done = f32[512,64,64]{2,1,0:T(8,128)} async-done(((f32[32,64,64]{2,1,0:T(8,128)}), f32[512,64,64]{2,1,0:T(8,128)}) %all-gather.6.cloned.1.call-update) | async-done | bytes 8388624 | tf_op jit(solution)/shard_map/all_gather | solution.py:24
  137.4 1.9 fusion.7
  140.9 42.5 %reduce-scatter.2.cloned.1.call-done = f32[2048,64]{0,1:T(8,128)} async-done(((f32[4096,64]{0,1:T(8,128)}), f32[2048,64]{0,1:T(8,128)}) %reduce-scatter.2.cloned.1.call-update) | async-done | bytes 524304 | tf_op jit(solution)/shard_map/reduce_scatter | solution.py:129
  183.4 1.6 fusion.4
  185.8 90.6 %all-reduce.2.cloned.1.call-done = f32[2048,64]{0,1:T(8,128)} async-done(((f32[2048,64]{0,1:T(8,128)}), f32[2048,64]{0,1:T(8,128)}) %all-reduce.2.cloned.1.call-update) | async-done | bytes 524304 | tf_op jit(solution)/shard_map/psum | solution.py:130
  276.4 2.7 multiply_subtract_fusion
  279.2 125.0 %all-gather.8.cloned.1.call-done = f32[512,64,64]{2,1,0:T(8,128)} async-done(((f32[32,64,64]{2,1,0:T(8,128)}), f32[512,64,64]{2,1,0:T(8,128)}) %all-gather.8.cloned.1.call-update) | async-done | bytes 8388624 | tf_op jit(solution)/shard_map/all_gather | solution.py:24
  404.3 22.4 %while.27 = (s32[]{:T(128)}, f32[32,64,64]{2,1,0:T(8,128)S(1)}, s32[]{:T(128)}, f32[16,32]{1,0:T(8,128)S(1)}, f32[16,32,64,64]{3,2,1,0:T(8,128)}, /*index=5*/s32[]{:T(128)}, s32[]{:T(128)}, s32[]{:T(128)}) while((s32[]{:T(128)}, f32[32,64,64]{2,1,0:T(8,128)S(1)}, s32[]{:T(128)}, f32[16,32]{1,0:T(8,128)S(1)}, f32[16,32,64,64]{3,2,1,0:T(8,128)}, ...), condition=%wide.region_4.5_spmd, body=%wide.region_3.4_spmd.sunk | while | flops 262149 | bytes 1573375 | solution.py:33
  404.3 1.4 bitcast_add_fusion.5
  405.8 1.4 bitcast_add_fusion.5
  407.3 1.4 bitcast_add_fusion.5
  408.8 1.4 bitcast_add_fusion.5
  410.3 1.4 bitcast_add_fusion.5
  411.8 1.4 bitcast_add_fusion.5
  413.3 1.4 bitcast_add_fusion.5
  414.8 1.4 bitcast_add_fusion.5
  416.3 1.4 bitcast_add_fusion.5
  417.8 1.4 bitcast_add_fusion.5
  419.3 1.4 bitcast_add_fusion.5
  420.8 1.4 bitcast_add_fusion.5
  (76 shorter events, 14.3 us)
Async XLA Ops:
  7.2 12.6 %copy-start = (bf16[1,128,4096]{2,1,0:T(8,128)(2,1)S(1)}, bf16[1,128,4096]{2,1,0:T(8,128)(2,1)}, u32[]{:S(2)}) copy-start(bf16[1,128,4096]{2,1,0:T(8,128)(2,1)} %param.12) | copy-start | bytes 3145732
  7.2 2.6 copy-start.5
  7.2 129.4 %all-gather.6.cloned.1.call-start = ((), (), s32[]{:S(2)}) async-start(), calls=%async_computation.3 | async-start | bytes 17825792 | tf_op jit(solution)/shard_map/all_gather | solution.py:24
  9.7 29.2 %copy-start.1 = (bf16[1,128,2048]{1,2,0:T(8,128)(2,1)}, bf16[1,128,2048]{1,2,0:T(8,128)(2,1)S(1)}, u32[]{:S(2)}) copy-start(bf16[1,128,2048]{1,2,0:T(8,128)(2,1)S(1)} %copy.44) | copy-start | bytes 1572868
  9.7 1.9 copy-start.4
  9.8 2.0 copy-start.3
  11.5 171.9 %reduce-scatter.2.cloned.1.call-start = ((), (), s32[]{:S(2)}) async-start(), calls=%async_computation.1 | async-start | bytes 1572864 | tf_op jit(solution)/shard_map/reduce_scatter | solution.py:129
  140.8 135.6 %all-reduce.2.cloned.1.call-start = ((), (), s32[]{:S(2)}) async-start(), calls=%async_computation.2 | async-start | bytes 1048576 | tf_op jit(solution)/shard_map/psum | solution.py:130
  183.4 220.8 %all-gather.8.cloned.1.call-start = ((), (), s32[]{:S(2)}) async-start(), calls=%async_computation.4 | async-start | bytes 17825792 | tf_op jit(solution)/shard_map/all_gather | solution.py:24
  426.8 1.0 copy-start.2
Sparse Core Ops, SparseCore 0:
  11.6 124.9 all-gather.5
  140.9 42.3 reduce-scatter.1
  186.8 89.6 all-reduce.1
  278.4 125.7 all-gather.7
where the time goes:
time: 437 us; the launch traced here: 436 us
  waiting for transfers between devices  354 us (81%)
  other arithmetic  26.4 us (6%)
  blocking collectives  26.2 us (6%)
  between operations  14 us (3%)
  matrix products  10.4 us (2%)
    all_gather x2, waiting for transfers between devices, entering(): gathered = jax.tree.map(lambda a: lax.all_gather(a, axis), part)  221 us
    psum x1, waiting for transfers between devices, on_device(): grad_rows = lax.psum(owner_grad, 'seq')  90.6 us
    reduce_scatter x1, waiting for transfers between devices, on_device(): lax.psum_scatter(partial_grad, 'dp', scatter_dimension=0, tiled=True)  42.5 us
    add x15, other arithmetic, pair_combine(): later_pair[0][:, None, None] * earlier_pair[1] + later_pair[1]  21.7 us
    all_gather x1, blocking collectives, entering(): gathered = jax.tree.map(lambda a: lax.all_gather(a, axis), part)  18.4 us
  transfers between devices with their start and end apart: 4, of which 4 were waited for; matrix products, arithmetic and copies ran while one was open for 2% of the time, Pallas kernels for 0%

commit v1 on v0

v1 whole, which is shorter than its diff:
```python
import functools

import jax
import jax.numpy as jnp
from jax import lax
from jax.experimental import pallas as pl
from jax.experimental.pallas import tpu as pltpu
from jax.sharding import PartitionSpec as P

HEAD_DIM = 64

beta_one = 0.9
beta_two = 0.999
adam_count = 10.0
learn_rate = 0.01
weight_decay = 0.1
epsilon = 1e-08
highest = lax.Precision.HIGHEST
f32 = jnp.float32
bf16 = jnp.bfloat16
MESH = pl.DeviceIdType.MESH
VMEM = pl.BlockSpec(memory_space=pltpu.VMEM)


def remote(src, dst, send_sem, recv_sem, where):
    return pltpu.make_async_remote_copy(
        src_ref=src, dst_ref=dst, send_sem=send_sem, recv_sem=recv_sem, device_id=where,
        device_id_type=MESH,
    )


def loop(low, high, body):
    lax.fori_loop(low, high, lambda i, carry: (body(i), carry)[1], 0)


class Scan:
    def __init__(self, count, me, local, decay, gathered, sent, result, sems):
        self.count, self.me = count, me
        self.local, self.decay, self.gathered, self.sent, self.result = (
            local, decay, gathered, sent, result)
        self.width = local.shape[1] // count
        self.out_send, self.out_recv, self.back_send, self.back_recv = sems

    def columns(self, place):
        return pl.ds(pl.multiple_of(place * self.width, self.width), self.width)

    def outward(self, j, source):
        return remote(self.local.at[:, self.columns(j)], self.gathered.at[source],
                      self.out_send.at[j], self.out_recv.at[source], {"seq": j})

    def homeward(self, i, owner):
        return remote(self.sent.at[i], self.result.at[:, self.columns(owner)],
                      self.back_send.at[i], self.back_recv.at[owner], {"seq": i})

    def start(self):
        loop(1, self.count,
             lambda k: self.outward(lax.rem(self.me + k, self.count), self.me).start())
        self.gathered[self.me] = self.local[:, self.columns(self.me)]

    def combine(self, reverse):
        count, me = self.count, self.me

        def one(k, running):
            i = count - 1 - k if reverse else k

            @pl.when(i != me)
            def _():
                self.outward(i, i).wait_recv()

            self.sent[i] = running.astype(bf16)
            new = self.decay[i] * running + self.gathered[i].astype(f32)

            @pl.when(i != me)
            def _():
                self.homeward(i, me).start()

            return new

        lax.fori_loop(0, count, one, jnp.zeros(self.gathered.shape[1:], f32))
        self.result[:, self.columns(me)] = self.sent[me]

    def finish(self):
        def one(k):
            j = lax.rem(self.me + k, self.count)
            self.outward(j, j).wait_send()
            self.homeward(j, j).wait_send()
            self.homeward(j, j).wait_recv()

        loop(1, self.count, one)


def greet(seq_count, dp_count, same_core):
    seq_me, dp_me = lax.axis_index("seq"), lax.axis_index("dp")
    barrier = pltpu.get_barrier_semaphore()
    loop(1, seq_count, lambda k: pl.semaphore_signal(
        barrier, inc=1, device_id={"seq": lax.rem(seq_me + k, seq_count)}, device_id_type=MESH))
    total = seq_count - 1
    places = seq_count // 2 if same_core else 1

    def over(k):
        d = lax.rem(dp_me + 1 + k // places, dp_count)
        s = lax.rem(seq_me + 2 * (k % places), seq_count)
        pl.semaphore_signal(barrier, inc=1, device_id={"seq": s, "dp": d}, device_id_type=MESH)

    loop(0, (dp_count - 1) * places, over)
    pl.semaphore_wait(barrier, total + (dp_count - 1) * places)


def first_kernel(seq_count, dp_count, weight, local, decay, weights, decays, result,
                 gathered, sent, w_send, w_recv, p_send, p_recv, d_send, d_recv,
                 a_send, a_recv, b_send, b_recv):
    seq_me, dp_me = lax.axis_index("seq"), lax.axis_index("dp")
    core = lax.rem(seq_me, 2)
    partner = seq_me + 1 - 2 * core
    greet(seq_count, dp_count, False)

    def across(d, source):
        return remote(weight.at[core], weights.at[source, core], w_send.at[d], w_recv.at[source],
                      {"dp": d})

    def beside(d, half):
        return remote(weights.at[d, half], weights.at[d, half], p_send.at[d], p_recv.at[d],
                      {"seq": partner})

    def tell(j, source):
        return remote(decay.at[j], decays.at[source], d_send.at[j], d_recv.at[source], {"seq": j})

    loop(1, dp_count, lambda k: across(lax.rem(dp_me + k, dp_count), dp_me).start())
    loop(1, seq_count, lambda k: tell(lax.rem(seq_me + k, seq_count), seq_me).start())
    scan = Scan(seq_count, seq_me, local, decays, gathered, sent, result,
                (a_send, a_recv, b_send, b_recv))
    scan.start()
    decays[seq_me] = decay[seq_me]
    weights[dp_me] = weight[...]

    def told(k):
        j = lax.rem(seq_me + k, seq_count)
        tell(j, j).wait_recv()

    loop(1, seq_count, told)

    def pass_on(k):
        d = lax.rem(dp_me + k, dp_count)
        across(d, d).wait_recv()
        beside(d, core).start()

    loop(1, dp_count, pass_on)
    scan.combine(True)

    def end(k):
        d = lax.rem(dp_me + k, dp_count)
        across(d, d).wait_send()
        beside(d, core).wait_send()
        beside(d, 1 - core).wait_recv()

    loop(1, dp_count, end)
    loop(1, seq_count, lambda k: tell(lax.rem(seq_me + k, seq_count), 0).wait_send())
    scan.finish()


def second_kernel(seq_count, local, decays, result, gathered, sent, a_send, a_recv, b_send, b_recv):
    greet(seq_count, 1, False)
    scan = Scan(seq_count, lax.axis_index("seq"), local, decays, gathered, sent, result,
                (a_send, a_recv, b_send, b_recv))
    scan.start()
    scan.combine(False)
    scan.finish()


def third_kernel(seq_count, dp_count, part, total, halves, summed, pieces,
                 h_send, h_recv, s_send, s_recv, g_send, g_recv):
    seq_me, dp_me = lax.axis_index("seq"), lax.axis_index("dp")
    core = lax.rem(seq_me, 2)
    chip = seq_me // 2
    partner = seq_me + 1 - 2 * core
    group = (seq_count // 2) * dp_count
    mine = chip * dp_count + dp_me
    greet(seq_count, dp_count, True)

    def half(g):
        return remote(part.at[1 - core, g], halves.at[g], h_send.at[g], h_recv.at[g],
                      {"seq": partner})

    def scatter(g, source):
        return remote(summed.at[g], pieces.at[source], s_send.at[g], s_recv.at[source],
                      {"seq": 2 * (g // dp_count) + core, "dp": g % dp_count})

    def share(j, source):
        return remote(total.at[seq_me], total.at[source], g_send.at[j], g_recv.at[source],
                      {"seq": j})

    loop(1, group + 1, lambda k: half(lax.rem(mine + k, group)).start())

    def pair(k):
        g = lax.rem(mine + k, group)
        half(g).wait_recv()
        summed[g] = (part[core, g].astype(f32) + halves[g].astype(f32)).astype(bf16)

        @pl.when(g != mine)
        def _():
            scatter(g, mine).start()

    loop(1, group + 1, pair)

    def collect(k, running):
        g = lax.rem(mine + group - k, group)
        scatter(g, g).wait_recv()
        return running + pieces[g].astype(f32)

    own = part[core, mine].astype(f32) + halves[mine].astype(f32)
    total[seq_me] = lax.fori_loop(1, group, collect, own).astype(bf16)
    loop(1, seq_count, lambda k: share(lax.rem(seq_me + k, seq_count), seq_me).start())

    def end(k):
        j = lax.rem(seq_me + seq_count - k, seq_count)
        share(j, j).wait_recv()
        share(j, j).wait_send()

    loop(1, group + 1, lambda k: half(lax.rem(mine + k, group)).wait_send())
    loop(1, group, lambda k: scatter(lax.rem(mine + k, group), 0).wait_send())
    loop(1, seq_count, end)


def dma(*sizes):
    return [pltpu.SemaphoreType.DMA((size,)) for size in sizes for _ in range(2)]


def adam_update(grad_rows, weight_rows, first_rows, second_rows):
    new_first = beta_one * first_rows + (1.0 - beta_one) * grad_rows
    new_second = beta_two * second_rows + (1.0 - beta_two) * grad_rows * grad_rows
    first_hat = new_first / (1.0 - beta_one**adam_count)
    second_hat = new_second / (1.0 - beta_two**adam_count)
    new_weight = weight_rows - learn_rate * (
        first_hat / (jnp.sqrt(second_hat) + epsilon) + weight_decay * weight_rows
    )
    return (new_weight, new_first, new_second)


def on_device(
    layer_input,
    scan_input,
    readout,
    log_decay,
    output_cotangent,
    write_weight,
    first_moment,
    second_moment,
):
    seq_count, dp_count = lax.axis_size("seq"), lax.axis_size("dp")
    input_rows = layer_input[0]
    scan_rows = scan_input[0]
    read_rows = readout[0]
    decay_rows = log_decay[0]
    back_rows = output_cotangent[0]
    length, model = input_rows.shape
    heads = decay_rows.shape[1]
    channels = scan_rows.shape[1]
    state_size = read_rows.shape[1]
    own_rows = write_weight.shape[0]
    width = channels // seq_count

    running = jnp.cumsum(decay_rows, axis=0)
    overall = running[-1]
    to_end = jnp.exp(overall[None, :] - running)
    from_start = jnp.exp(running)
    decay_total = jnp.exp(overall)

    def widen(a):
        return jnp.repeat(a, HEAD_DIM, axis=1)

    scaled_scan = scan_rows.astype(f32) * widen(to_end)
    scaled_back = back_rows.astype(f32) * widen(from_start)

    def state_of(vectors, rows):
        return lax.dot_general(
            vectors.astype(f32), rows, (((0,), (0,)), ((), ())), precision=highest
        ).astype(bf16)

    reverse_local = state_of(read_rows, scaled_back)
    decay_lanes = widen(decay_total[None]).reshape(seq_count, 1, width)
    weight_half = write_weight.T.astype(bf16).reshape(2, state_size // 2, own_rows)
    exchange = [
        pltpu.VMEM((seq_count, state_size, width), bf16),
        pltpu.VMEM((seq_count, state_size, width), bf16),
    ]
    weights, decays, grad_after = pl.pallas_call(
        functools.partial(first_kernel, seq_count, dp_count),
        out_shape=(
            jax.ShapeDtypeStruct((dp_count,) + weight_half.shape, bf16),
            jax.ShapeDtypeStruct(decay_lanes.shape, f32),
            jax.ShapeDtypeStruct((state_size, channels), bf16),
        ),
        in_specs=[VMEM] * 3,
        out_specs=[VMEM] * 3,
        scratch_shapes=exchange + dma(dp_count, dp_count, seq_count, seq_count, seq_count),
        compiler_params=pltpu.CompilerParams(collective_id=0, has_side_effects=True),
        name="gather_reverse",
    )(weight_half, reverse_local, decay_lanes)

    weight_all = weights.reshape(dp_count, state_size, own_rows).transpose(1, 0, 2)
    write_half = lax.dot_general(
        input_rows, weight_all.reshape(state_size, model), (((1,), (1,)), ((), ())),
        preferred_element_type=f32,
    ).astype(bf16)
    state_local = state_of(write_half, scaled_scan)
    state_before = pl.pallas_call(
        functools.partial(second_kernel, seq_count),
        out_shape=jax.ShapeDtypeStruct((state_size, channels), bf16),
        in_specs=[VMEM] * 2,
        out_specs=VMEM,
        scratch_shapes=exchange + dma(seq_count, seq_count),
        compiler_params=pltpu.CompilerParams(collective_id=1, has_side_effects=True),
        name="forward_states",
    )(state_local, decays)

    scan_split = scan_rows.reshape(length, heads, HEAD_DIM)
    back_split = back_rows.reshape(length, heads, HEAD_DIM)
    crossed = jnp.einsum("thp,shp->hts", scan_split, back_split, preferred_element_type=f32)
    heads_running = running.T
    spread = heads_running[:, None, :] - heads_running[:, :, None]
    row_index = lax.broadcasted_iota(jnp.int32, (length, length), 0)
    col_index = lax.broadcasted_iota(jnp.int32, (length, length), 1)
    kernel_mat = (
        jnp.where((row_index <= col_index)[None], jnp.exp(jnp.minimum(spread, 0.0)), 0.0) * crossed
    )
    kernel_sum = jnp.sum(kernel_mat, axis=0)
    write_grad = jnp.dot(kernel_sum, read_rows.astype(f32), precision=highest)
    write_grad = write_grad + lax.dot_general(
        scaled_scan.astype(bf16), grad_after, (((1,), (1,)), ((), ())), preferred_element_type=f32
    )
    grad_half = write_grad.astype(bf16)
    partial = lax.dot_general(
        grad_half, input_rows, (((0,), (0,)), ((), ())), preferred_element_type=f32
    ).astype(bf16)
    chips = seq_count // 2
    part = partial.reshape(state_size, dp_count, chips, 2, own_rows // seq_count)
    piece = (state_size * own_rows // seq_count // 128, 128)
    part = part.transpose(3, 2, 1, 0, 4).reshape((2, chips * dp_count) + piece)
    grad_sum = pl.pallas_call(
        functools.partial(third_kernel, seq_count, dp_count),
        out_shape=jax.ShapeDtypeStruct((seq_count,) + piece, bf16),
        in_specs=[VMEM],
        out_specs=VMEM,
        scratch_shapes=[pltpu.VMEM((chips * dp_count,) + piece, bf16)] * 3
        + dma(chips * dp_count, chips * dp_count, seq_count),
        compiler_params=pltpu.CompilerParams(collective_id=2, has_side_effects=True),
        name="reduce_gradient",
    )(part)
    grad_rows = grad_sum.reshape(seq_count, state_size, own_rows // seq_count).transpose(1, 0, 2)
    grad_rows = grad_rows.reshape(state_size, own_rows).astype(f32).T
    new_weight, new_first, new_second = adam_update(
        grad_rows, write_weight, first_moment, second_moment
    )

    def per_head(a):
        return jnp.sum(a.reshape(a.shape[0], heads, HEAD_DIM), axis=2)

    term_one = decay_total * jnp.sum(
        per_head(grad_after.astype(f32) * state_before.astype(f32)), axis=0)
    grad_write = jnp.dot(write_half, grad_after, preferred_element_type=f32)
    second_rows = to_end * per_head(scan_rows.astype(f32) * grad_write)
    term_two = jnp.cumsum(second_rows, axis=0) - second_rows
    state_read = jnp.dot(read_rows, state_before, preferred_element_type=f32)
    third_rows = from_start * per_head(back_rows.astype(f32) * state_read)
    term_three = jnp.flip(jnp.cumsum(jnp.flip(third_rows, 0), axis=0), 0)
    write_read = jnp.dot(write_half, read_rows.T, preferred_element_type=f32)
    pairing = jnp.where((row_index < col_index)[None], kernel_mat * write_read[None], 0.0)
    balance = (jnp.sum(pairing, axis=2) - jnp.sum(pairing, axis=1)).T
    term_four = jnp.cumsum(balance, axis=0) - balance
    decay_grad = term_one[None, :] + term_two + term_three + term_four
    return (decay_grad[None], new_weight, new_first, new_second)


def solution(mesh):
    in_specs = (
        P("dp", "seq", None),
        P("dp", "seq", None),
        P("dp", "seq", None),
        P("dp", "seq", None),
        P("dp", "seq", None),
        P("dp", None),
        P("dp", None),
        P("dp", None),
    )
    out_specs = (P("dp", "seq", None), P("dp", None), P("dp", None), P("dp", None))
    return jax.shard_map(
        on_device, mesh=mesh, in_specs=in_specs, out_specs=out_specs, check_vma=False
    )
```

time: 437 us -> 94.5 us (0.22)
  the two profiles are of different devices: /device:TPU:29 before, /device:TPU:0 now
where the time goes in v1:
time: 94.5 us; the launch traced here: 94 us
  Pallas kernels  64.3 us (68%)
  local copies, waits for them, and re-layouts  12.7 us (13%)
  matrix products  9.9 us (10%)
  other arithmetic  6.27 us (7%)
    pallas_call x1, Pallas kernels, on_device(): pl.pallas_call(functools.partial(first_kernel, seq_count, dp_count), out_...  25.2 us
    pallas_call x1, Pallas kernels, on_device(): pl.pallas_call(functools.partial(third_kernel, seq_count, dp_count), out_...  24 us
    pallas_call x1, Pallas kernels, on_device(): pl.pallas_call(functools.partial(second_kernel, seq_count), out_shape=jax...  15 us
    dot_general x2, matrix products, state_of(): lax.dot_general(vectors.astype(f32), rows, (((0,), (0,)), ((), ())), prec...  2.73 us
    sub x1, other arithmetic, adam_update(): weight_rows - learn_rate * (first_hat / (jnp.sqrt(second_hat) + epsilon)...  2.35 us
    dot_general x1, matrix products, on_device(): lax.dot_general(grad_half, input_rows, (((0,), (0,)), ((), ())), preferre...  2.12 us

profile of v1, /device:TPU:0, one launch (start us, length us, event | category | flops | bytes accessed | tf_op | source)
XLA Modules:
  0.0 94.0 jit_solution(11872152651271833331)
XLA Ops:
  0.7 1.0 %copy.70 = f32[128,32]{1,0:T(8,128)S(1)} copy(f32[128,32]{0,1:T(8,128)} %bitcast.117) | data formatting | bytes 32768 | tf_op jit(solution)/shard_map/squeeze | solution.py:253
  1.8 0.5 slice_bitcast_fusion
  2.5 0.7 broadcast_in_dim.39.decay
  3.3 0.7 copy.74
  4.0 0.8 convert_element_type.66
  5.5 0.6 copy-done.10
  6.1 1.4 %fusion.1.local = bf16[64,2048]{1,0:T(8,128)(2,1)} fusion(f32[128,2048]{0,1:T(8,128)S(1)} %bitcast.106, bf16[1,128,64]{1,2,0:T(8,128)(2,1)S(1)} %copy-done.10), kind=kOutput, calls=%fused_computation.6 | convolution fusion | flops 201457664 | bytes 1327104 | tf_op jit(solution)/shard_map/dot_general | solution.py:275
  7.5 25.2 %gather_reverse.1 = (bf16[2,2,32,2048]{3,2,1,0:T(8,128)(2,1)}, f32[16,1,128]{2,1,0:T(1,128)}, bf16[64,2048]{1,0:T(8,128)(2,1)}) custom-call(bf16[2,32,2048]{2,1,0:T(8,128)(2,1)} %bitcast.114, bf16[64,2048]{1,0:T(8,128)(2,1)} %fusion.1.local, f32[16,1,128]{2,1,0:T(1,128)} %broadcast_in_dim.39.decay), custom_call_target="tpu_custom_call" | custom-call | tf_op jit(solution)/shard_map/gather_reverse/pallas_call | solution.py:286
  32.8 1.6 %copy.73 = bf16[2,64,2048]{2,0,1:T(2,128)(2,1)S(1)} copy(bf16[2,64,2048]{2,1,0:T(8,128)(2,1)} %bitcast.116) | data formatting | bytes 1048576 | tf_op jit(solution)/shard_map/reshape | solution.py:300
  35.2 1.9 %fusion.2 = (f32[32,128]{1,0:T(8,128)S(1)}, f32[32,128]{1,0:T(8,128)S(1)}, f32[128,128]{1,0:T(8,128)S(1)}) fusion(f32[128,128]{1,0:T(8,128)S(1)} %fusion.18, pred[128,128]{1,0:T(8,128)(4,1)S(1)} %get-tuple-element.37, bf16[128,32,64]{0,2,1:T(8,128)(2,1)S(1)} %bitcast.115, bf16[128,32,64]{0,2,1:T(8,128)(2,1)S(1)} %bitcast.109, f32[32,128]{1,0:T(8,128)S(1)} %copy.82, ...), kind=kOutput, calls=%fused_computation.9 | convolution fusion | flops 71802880 | bytes 1261568 | tf_op jit(solution)/shard_map/thp,shp->hts/dot_general | solution.py:318
  37.1 0.8 fusion.16
  38.6 1.3 %copy.76 = f32[128,2048]{0,1:T(8,128)} copy(f32[128,2048]{1,0:T(8,128)S(1)} %convolution_multiply_fusion) | data formatting | bytes 2097152 | tf_op jit(solution)/shard_map/mul | solution.py:361
  39.9 1.3 %bitcast_reduce_fusion.1 = f32[128,32]{0,1:T(8,128)S(1)} fusion(f32[128,2048]{0,1:T(8,128)} %copy.76), kind=kLoop, calls=%fused_computation.16 | loop fusion | flops 258048 | bytes 1064960 | tf_op jit(solution)/shard_map/reduce_sum | solution.py:356
  41.6 0.7 copy.78
  42.3 1.1 %broadcast_in_dim.40 = f32[128,32,64]{0,2,1:T(8,128)} broadcast(f32[128,32]{0,1:T(8,128)S(1)} %get-tuple-element.33), dimensions={0,1} | broadcast | bytes 1064960 | tf_op jit(solution)/shard_map/broadcast_in_dim | solution.py:269
  43.4 1.6 %copy.75 = f32[128,2048]{1,0:T(8,128)S(1)} copy(f32[128,2048]{0,1:T(8,128)} %bitcast.107) | data formatting | bytes 2097152 | tf_op jit(solution)/shard_map/reshape | solution.py:269
  44.9 1.3 %convolution_convert_fusion.1.local = bf16[64,2048]{1,0:T(8,128)(2,1)} fusion(bf16[64,128]{1,0:T(8,128)(2,1)S(1)} %convolution_convert_fusion.3, f32[128,2048]{1,0:T(8,128)S(1)} %copy.75, bf16[1,128,2048]{2,1,0:T(8,128)(2,1)S(1)} %copy-done.1), kind=kOutput, calls=%fused_computation.4 | convolution fusion | flops 201981952 | bytes 1851392 | tf_op jit(solution)/shard_map/dot_general | solution.py:275
  46.2 2.1 %convolution_convert_fusion = bf16[64,4096]{1,0:T(8,128)(2,1)} fusion(f32[128,64]{0,1:T(8,128)} %fusion.16, bf16[64,2048]{1,0:T(8,128)(2,1)S(1)} %copy-done.2, bf16[1,128,4096]{2,1,0:T(8,128)(2,1)S(1)} %copy-done, f32[128,2048]{1,0:T(8,128)S(1)} %copy.75, bf16[1,128,2048]{2,1,0:T(8,128)(2,1)S(1)} %copy-done.1), kind=kOutput, calls=%fused_computation | convolution fusion | flops 101728256 | bytes 3440640 | tf_op jit(solution)/shard_map/dot_general | solution.py:332
  48.3 15.0 %forward_states.1 = bf16[64,2048]{1,0:T(8,128)(2,1)} custom-call(bf16[64,2048]{1,0:T(8,128)(2,1)} %convolution_convert_fusion.1.local, f32[16,1,128]{2,1,0:T(1,128)} %get-tuple-element.9.decays), custom_call_target="tpu_custom_call" | custom-call | tf_op jit(solution)/shard_map/forward_states/pallas_call | solution.py:306
  63.4 1.4 %bitcast_reduce_fusion = f32[128,32]{0,1:T(8,128)S(1)} fusion(bf16[64,2048]{1,0:T(8,128)(2,1)} %forward_states.1, bf16[1,128,2048]{1,2,0:T(8,128)(2,1)S(1)} %copy.71, bf16[1,128,64]{1,2,0:T(8,128)(2,1)S(1)} %copy-done.10), kind=kOutput, calls=%fused_computation.15 | convolution fusion | flops 34336768 | bytes 819200 | tf_op jit(solution)/shard_map/dot_general | solution.py:363
  65.3 1.0 %copy.87 = bf16[64,2,8,2,128]{4,0,1,2,3:T(8,128)(2,1)} copy(bf16[64,2,8,2,128]{4,3,2,1,0:T(2,128)(2,1)S(1)} %reshape.90) | data formatting | bytes 1048576 | tf_op jit(solution)/shard_map/reshape | solution.py:336
  66.3 24.0 %reduce_gradient.1 = bf16[16,64,128]{2,1,0:T(8,128)(2,1)} custom-call(bf16[2,16,64,128]{3,2,1,0:T(8,128)(2,1)} %bitcast.112), custom_call_target="tpu_custom_call" | custom-call | tf_op jit(solution)/shard_map/reduce_gradient/pallas_call | solution.py:339
  90.9 0.7 add_bitcast_fusion
  91.6 2.4 %multiply_subtract_fusion = (f32[2048,64]{0,1:T(8,128)}, f32[2048,64]{0,1:T(8,128)}, f32[2048,64]{0,1:T(8,128)}) fusion(f32[2048,64]{0,1:T(8,128)S(1)} %copy-done.4, f32[2048,64]{0,1:T(8,128)S(1)} %copy-done.8, f32[2048,64]{0,1:T(8,128)S(1)} %copy-done.9, bf16[16,64,128]{2,1,0:T(8,128)(2,1)} %reduce_gradient.1), kind=kLoop, calls=%fused_computation.29 | loop fusion | flops 2097152 | bytes 3407872 | tf_op jit(solution)/shard_map/sub | solution.py:233
  (59 shorter events, 4.1 us)
Async XLA Ops:
  0.6 33.9 %copy-start = (bf16[1,128,4096]{2,1,0:T(8,128)(2,1)S(1)}, bf16[1,128,4096]{2,1,0:T(8,128)(2,1)}, u32[]{:S(2)}) copy-start(bf16[1,128,4096]{2,1,0:T(8,128)(2,1)} %param.8) | copy-start | bytes 3145732
  0.6 3.4 %copy-start.3 = (f32[2048,64]{0,1:T(8,128)S(1)}, f32[2048,64]{0,1:T(8,128)}, u32[]{:S(2)}) copy-start(f32[2048,64]{0,1:T(8,128)} %param.13) | copy-start | bytes 1572868
  0.7 4.1 %copy-start.7 = (bf16[1,128,2048]{2,1,0:T(8,128)(2,1)S(1)}, bf16[1,128,2048]{2,1,0:T(8,128)(2,1)}, u32[]{:S(2)}) copy-start(bf16[1,128,2048]{2,1,0:T(8,128)(2,1)} %param.12) | copy-start | bytes 1572868
  3.3 1.8 %copy-start.1 = (bf16[1,128,2048]{2,1,0:T(8,128)(2,1)S(1)}, bf16[1,128,2048]{2,1,0:T(8,128)(2,1)}, u32[]{:S(2)}) copy-start(bf16[1,128,2048]{2,1,0:T(8,128)(2,1)} %param.9) | copy-start | bytes 1572868
  5.4 0.7 copy-start.10
  35.2 3.0 %copy-start.2 = (bf16[64,2048]{1,0:T(8,128)(2,1)S(1)}, bf16[64,2048]{1,0:T(8,128)(2,1)}, u32[]{:S(2)}) copy-start(bf16[64,2048]{1,0:T(8,128)(2,1)} %get-tuple-element.7) | copy-start | bytes 786436
  39.9 1.3 %copy-start.11 = (f32[128,32]{0,1:T(8,128)S(1)}, f32[128,32]{0,1:T(8,128)}, u32[]{:S(2)}) copy-start(f32[128,32]{0,1:T(8,128)} %copy.74) | copy-start | bytes 49156
  39.9 1.3 %copy-start.13 = (f32[32]{0:T(128)S(1)}, f32[32]{0:T(128)}, u32[]{:S(2)}) copy-start(f32[32]{0:T(128)} %get-tuple-element.34) | copy-start | bytes 388
  48.3 16.5 %copy-start.5 = (bf16[64,4096]{1,0:T(8,128)(2,1)S(1)}, bf16[64,4096]{1,0:T(8,128)(2,1)}, u32[]{:S(2)}) copy-start(bf16[64,4096]{1,0:T(8,128)(2,1)} %convolution_convert_fusion) | copy-start | bytes 1572868
  63.4 1.4 %copy-start.6 = (bf16[64,2048]{1,0:T(8,128)(2,1)S(1)}, bf16[64,2048]{1,0:T(8,128)(2,1)}, u32[]{:S(2)}) copy-start(bf16[64,2048]{1,0:T(8,128)(2,1)} %forward_states.1) | copy-start | bytes 786436
  65.3 25.7 %copy-start.12 = (f32[128,32]{0,1:T(8,128)S(1)}, f32[128,32]{0,1:T(8,128)}, u32[]{:S(2)}) copy-start(f32[128,32]{0,1:T(8,128)} %copy.78) | copy-start | bytes 49156
  66.3 25.4 %copy-start.4 = (f32[2048,64]{0,1:T(8,128)S(1)}, f32[2048,64]{0,1:T(8,128)}, u32[]{:S(2)}) copy-start(f32[2048,64]{0,1:T(8,128)} %param.13) | copy-start | bytes 1572868
  66.3 25.4 %copy-start.8 = (f32[2048,64]{0,1:T(8,128)S(1)}, f32[2048,64]{0,1:T(8,128)}, u32[]{:S(2)}) copy-start(f32[2048,64]{0,1:T(8,128)} %param.14) | copy-start | bytes 1572868
  66.3 25.4 %copy-start.9 = (f32[2048,64]{0,1:T(8,128)S(1)}, f32[2048,64]{0,1:T(8,128)}, u32[]{:S(2)}) copy-start(f32[2048,64]{0,1:T(8,128)} %param.15) | copy-start | bytes 1572868

commit v2 on v1

--- a/solution.py
+++ b/solution.py
@@ -79,14 +79,24 @@
         lax.fori_loop(0, count, one, jnp.zeros(self.gathered.shape[1:], f32))
         self.result[:, self.columns(me)] = self.sent[me]
 
-    def finish(self):
+    def arrive(self):
+        def one(k):
+            j = lax.rem(self.me + k, self.count)
+            self.homeward(j, j).wait_recv()
+
+        loop(1, self.count, one)
+
+    def drain(self):
         def one(k):
             j = lax.rem(self.me + k, self.count)
             self.outward(j, j).wait_send()
             self.homeward(j, j).wait_send()
-            self.homeward(j, j).wait_recv()
 
         loop(1, self.count, one)
+
+    def finish(self):
+        self.arrive()
+        self.drain()
 
 
 def greet(seq_count, dp_count, same_core):
@@ -103,7 +113,7 @@
         pl.semaphore_signal(barrier, inc=1, device_id={"seq": s, "dp": d}, device_id_type=MESH)
 
     loop(0, (dp_count - 1) * places, over)
-    pl.semaphore_wait(barrier, total + (dp_count - 1) * places)
+    return lambda: pl.semaphore_wait(barrier, total + (dp_count - 1) * places)
 
 
 def first_kernel(seq_count, dp_count, weight, local, decay, weights, decays, result,
@@ -112,7 +122,7 @@
     seq_me, dp_me = lax.axis_index("seq"), lax.axis_index("dp")
     core = lax.rem(seq_me, 2)
     partner = seq_me + 1 - 2 * core
-    greet(seq_count, dp_count, False)
+    greet(seq_count, dp_count, False)()
 
     def across(d, source):
         return remote(weight.at[core], weights.at[source, core], w_send.at[d], w_recv.at[source],
@@ -159,7 +169,7 @@
 
 
 def second_kernel(seq_count, local, decays, result, gathered, sent, a_send, a_recv, b_send, b_recv):
-    greet(seq_count, 1, False)
+    greet(seq_count, 1, False)()
     scan = Scan(seq_count, lax.axis_index("seq"), local, decays, gathered, sent, result,
                 (a_send, a_recv, b_send, b_recv))
     scan.start()
@@ -175,7 +185,7 @@
     partner = seq_me + 1 - 2 * core
     group = (seq_count // 2) * dp_count
     mine = chip * dp_count + dp_me
-    greet(seq_count, dp_count, True)
+    greet(seq_count, dp_count, True)()
 
     def half(g):
         return remote(part.at[1 - core, g], halves.at[g], h_send.at[g], h_recv.at[g],
@@ -216,6 +226,229 @@
         share(j, j).wait_recv()
         share(j, j).wait_send()
 
+    loop(1, group + 1, lambda k: half(lax.rem(mine + k, group)).wait_send())
+    loop(1, group, lambda k: scatter(lax.rem(mine + k, group), 0).wait_send())
+    loop(1, seq_count, end)
+
+
+def nt(a, b):
+    return lax.dot_general(a, b, (((1,), (1,)), ((), ())), preferred_element_type=f32)
+
+
+def split(a):
+    high = a.astype(bf16)
+    return high, (a - high.astype(f32)).astype(bf16)
+
+
+def exact(a, b):
+    return lax.dot_general(a, b, (((1,), (1,)), ((), ())), precision=highest)
+
+
+def one_kernel(seq_count, dp_count, weight_rows, log_decay, scan_rows, back_rows, read_rows,
+               input_rows, decay_grad, total,
+               grad_after, state_before, weight, reverse_local, decay, scaled_scan, kernel_mat,
+               row_sums, col_sums, weights, decays, forward_local, reverse_got, reverse_sent, forward_got,
+               forward_sent, part, halves, summed, pieces,
+               w_send, w_recv, p_send, p_recv, d_send, d_recv, a_send, a_recv, b_send, b_recv,
+               e_send, e_recv, f_send, f_recv, h_send, h_recv, s_send, s_recv, g_send, g_recv):
+    seq_me, dp_me = lax.axis_index("seq"), lax.axis_index("dp")
+    core = lax.rem(seq_me, 2)
+    chip = seq_me // 2
+    partner = seq_me + 1 - 2 * core
+    group = (seq_count // 2) * dp_count
+    mine = chip * dp_count + dp_me
+    ready = greet(seq_count, dp_count, True)
+    length, channels = scan_rows.shape
+    heads = channels // HEAD_DIM
+    state_size = read_rows.shape[0]
+    row_index = lax.broadcasted_iota(jnp.int32, (length, length), 0)
+    col_index = lax.broadcasted_iota(jnp.int32, (length, length), 1)
+    causal = row_index <= col_index
+    before = (col_index < row_index).astype(f32)
+    upto = (col_index <= row_index).astype(f32)
+    onward = causal.astype(f32)
+    run_cols = exact(upto, log_decay[...])
+    run_rows = exact(log_decay[...], upto)
+    overall = run_cols[length - 1 :, :]
+    to_end = jnp.exp(overall - run_cols)
+    from_start = jnp.exp(run_cols)
+    owner = lax.broadcasted_iota(jnp.int32, (heads, channels), 0)
+    spot = lax.broadcasted_iota(jnp.int32, (heads, channels), 1) - owner * HEAD_DIM
+    member = ((spot >= 0) & (spot < HEAD_DIM)).astype(bf16)
+
+    def widen(a):
+        high, low = split(a)
+        return (jnp.dot(high, member, preferred_element_type=f32)
+                + jnp.dot(low, member, preferred_element_type=f32))
+
+    def per_head(a):
+        high, low = split(a)
+        return nt(high, member) + nt(low, member)
+
+    back_high, back_low = split(back_rows[...].astype(f32) * widen(from_start))
+    reverse_local[...] = (
+        jnp.dot(read_rows[...], back_high, preferred_element_type=f32)
+        + jnp.dot(read_rows[...], back_low, preferred_element_type=f32)
+    ).astype(bf16)
+    decay_wide = widen(jnp.exp(jnp.broadcast_to(overall, (8, heads))))[:1]
+    width = channels // seq_count
+    for j in range(seq_count):
+        decay[j] = decay_wide[:, j * width : (j + 1) * width]
+    for side in range(2):
+        weight[side] = weight_rows[
+            side * state_size // 2 : (side + 1) * state_size // 2, :].astype(bf16)
+    ready()
+
+    def across(d, source):
+        return remote(weight.at[core], weights.at[source, core], w_send.at[d], w_recv.at[source],
+                      {"dp": d})
+
+    def beside(d, half):
+        return remote(weights.at[d, half], weights.at[d, half], p_send.at[d], p_recv.at[d],
+                      {"seq": partner})
+
+    def tell(j, source):
+        return remote(decay.at[j], decays.at[source], d_send.at[j], d_recv.at[source], {"seq": j})
+
+    def half(g):
+        return remote(part.at[1 - core, g], halves.at[g], h_send.at[g], h_recv.at[g],
+                      {"seq": partner})
+
+    def scatter(g, source):
+        return remote(summed.at[g], pieces.at[source], s_send.at[g], s_recv.at[source],
+                      {"seq": 2 * (g // dp_count) + core, "dp": g % dp_count})
+
+    def share(j, source):
+        return remote(total.at[seq_me], total.at[source], g_send.at[j], g_recv.at[source],
+                      {"seq": j})
+
+    loop(1, dp_count, lambda k: across(lax.rem(dp_me + k, dp_count), dp_me).start())
+    loop(1, seq_count, lambda k: tell(lax.rem(seq_me + k, seq_count), seq_me).start())
+    reverse = Scan(seq_count, seq_me, reverse_local, decays, reverse_got, reverse_sent, grad_after,
+                   (a_send, a_recv, b_send, b_recv))
+    forward = Scan(seq_count, seq_me, forward_local, decays, forward_got, forward_sent,
+                   state_before, (e_send, e_recv, f_send, f_recv))
+    reverse.start()
+    decays[seq_me] = decay[seq_me]
+    weights[dp_me] = weight[...]
+
+    kernel_sum = jnp.zeros((length, length), f32)
+    scaled_scan[...] = scan_rows[...].astype(f32) * widen(to_end)
+    for h in range(heads):
+        at = slice(h * HEAD_DIM, (h + 1) * HEAD_DIM)
+        crossed = nt(scan_rows[:, at], back_rows[:, at])
+        spread = run_rows[h : h + 1, :] - run_cols[:, h : h + 1]
+        term = jnp.where(causal, jnp.exp(jnp.minimum(spread, 0.0)), 0.0) * crossed
+        kernel_mat[h] = term
+        kernel_sum += term
+
+    def pass_on(k):
+        d = lax.rem(dp_me + k, dp_count)
+        across(d, d).wait_recv()
+        beside(d, core).start()
+
+    def told(k):
+        j = lax.rem(seq_me + k, seq_count)
+        tell(j, j).wait_recv()
+
+    loop(1, dp_count, pass_on)
+    loop(1, seq_count, told)
+    reverse.combine(True)
+
+    def beside_end(k):
+        d = lax.rem(dp_me + k, dp_count)
+        beside(d, 1 - core).wait_recv()
+
+    loop(1, dp_count, beside_end)
+    own_rows = weight.shape[2]
+    write = []
+    for side in range(2):
+        some = nt(weights[0, side], input_rows[:, :own_rows])
+        for d in range(1, dp_count):
+            some += nt(weights[d, side], input_rows[:, d * own_rows : (d + 1) * own_rows])
+        write.append(some)
+    write = jnp.concatenate(write, axis=0)
+    write_rows = write.T.astype(bf16)
+    write = write.astype(bf16)
+    step = channels // 4
+    for low in range(0, channels, step):
+        scan_high, scan_low = split(scaled_scan[:, low : low + step])
+        forward_local[:, low : low + step] = (
+            jnp.dot(write, scan_high, preferred_element_type=f32)
+            + jnp.dot(write, scan_low, preferred_element_type=f32)
+        ).astype(bf16)
+    forward.start()
+
+    reverse.arrive()
+    sum_high, sum_low = split(kernel_sum)
+    write_grad = nt(grad_after[...], scaled_scan[...].astype(bf16))
+    write_grad += nt(read_rows[...], sum_high) + nt(read_rows[...], sum_low)
+    grad_half = write_grad.astype(bf16)
+    wide = own_rows // seq_count
+    for g in range(group):
+        low = (g % dp_count) * own_rows + 2 * (g // dp_count) * wide
+        term = jnp.dot(grad_half, input_rows[:, low : low + 2 * wide],
+                       preferred_element_type=f32).astype(bf16)
+        part[0, g] = term[:, :wide]
+        part[1, g] = term[:, wide:]
+    loop(1, group + 1, lambda k: half(lax.rem(mine + k, group)).start())
+    forward.combine(False)
+
+    def pair(k):
+        g = lax.rem(mine + k, group)
+        half(g).wait_recv()
+        summed[g] = (part[core, g].astype(f32) + halves[g].astype(f32)).astype(bf16)
+
+        @pl.when(g != mine)
+        def _():
+            scatter(g, mine).start()
+
+    loop(1, group + 1, pair)
+
+    read_turned = read_rows[...].astype(f32).T.astype(bf16)
+    write_read = jnp.where(row_index < col_index, nt(write_rows, read_turned), 0.0)
+    for h in range(heads):
+        pairing = kernel_mat[h] * write_read
+        row_sums[:, h : h + 1] = jnp.sum(pairing, axis=1, keepdims=True)
+        col_sums[h : h + 1, :] = jnp.sum(pairing, axis=0, keepdims=True)
+    grad_write = jnp.dot(write_rows, grad_after[...], preferred_element_type=f32)
+    second = to_end * per_head(scan_rows[...].astype(f32) * grad_write) + row_sums[...]
+
+    def collect(k, running):
+        g = lax.rem(mine + group - k, group)
+        scatter(g, g).wait_recv()
+        return running + pieces[g].astype(f32)
+
+    own = part[core, mine].astype(f32) + halves[mine].astype(f32)
+    total[seq_me] = lax.fori_loop(1, group, collect, own).astype(bf16)
+    loop(1, seq_count, lambda k: share(lax.rem(seq_me + k, seq_count), seq_me).start())
+    forward.arrive()
+    state_read = jnp.dot(read_turned, state_before[...], preferred_element_type=f32)
+    third = from_start * per_head(back_rows[...].astype(f32) * state_read)
+    both = jnp.sum(grad_after[...].astype(f32) * state_before[...].astype(f32), axis=0,
+                   keepdims=True)
+    first = jnp.exp(overall) * per_head(jnp.broadcast_to(both, (8, channels)))[:1]
+    decay_grad[...] = (
+        first
+        + jnp.dot(before, second, precision=highest)
+        - exact(before, col_sums[...])
+        + jnp.dot(onward, third, precision=highest)
+    )
+
+    def end(k):
+        j = lax.rem(seq_me + seq_count - k, seq_count)
+        share(j, j).wait_recv()
+        share(j, j).wait_send()
+        tell(j, j).wait_send()
+
+    def dp_end(k):
+        d = lax.rem(dp_me + k, dp_count)
+        across(d, d).wait_send()
+        beside(d, core).wait_send()
+
+    loop(1, dp_count, dp_end)
+    reverse.drain()
+    forward.drain()
     loop(1, group + 1, lambda k: half(lax.rem(mine + k, group)).wait_send())
     loop(1, group, lambda k: scatter(lax.rem(mine + k, group), 0).wait_send())
     loop(1, seq_count, end)
@@ -259,115 +492,153 @@
     own_rows = write_weight.shape[0]
     width = channels // seq_count
 
-    running = jnp.cumsum(decay_rows, axis=0)
-    overall = running[-1]
-    to_end = jnp.exp(overall[None, :] - running)
-    from_start = jnp.exp(running)
-    decay_total = jnp.exp(overall)
-
-    def widen(a):
-        return jnp.repeat(a, HEAD_DIM, axis=1)
-
-    scaled_scan = scan_rows.astype(f32) * widen(to_end)
-    scaled_back = back_rows.astype(f32) * widen(from_start)
-
-    def state_of(vectors, rows):
-        return lax.dot_general(
-            vectors.astype(f32), rows, (((0,), (0,)), ((), ())), precision=highest
+    chips = seq_count // 2
+    group = chips * dp_count
+    if own_rows % (128 * seq_count) == 0:
+        piece = (state_size, own_rows // seq_count)
+        exchange = [pltpu.VMEM((seq_count, state_size, width), bf16)] * 2
+        states = pltpu.VMEM((state_size, channels), bf16)
+        halves = (2, state_size // 2, own_rows)
+        decay_grad, grad_sum = pl.pallas_call(
+            functools.partial(one_kernel, seq_count, dp_count),
+            out_shape=(
+                jax.ShapeDtypeStruct((length, heads), f32),
+                jax.ShapeDtypeStruct((seq_count,) + piece, bf16),
+            ),
+            in_specs=[VMEM] * 6,
+            out_specs=[VMEM] * 2,
+            scratch_shapes=[
+                states,
+                states,
+                pltpu.VMEM(halves, bf16),
+                states,
+                pltpu.VMEM((seq_count, 1, width), f32),
+                pltpu.VMEM((length, channels), f32),
+                pltpu.VMEM((heads, length, length), f32),
+                pltpu.VMEM((length, heads), f32),
+                pltpu.VMEM((heads, length), f32),
+                pltpu.VMEM((dp_count,) + halves, bf16),
+                pltpu.VMEM((seq_count, 1, width), f32),
+                states,
+            ]
+            + exchange
+            + exchange
+            + [pltpu.VMEM((2, group) + piece, bf16)]
+            + [pltpu.VMEM((group,) + piece, bf16)] * 3
+            + dma(dp_count, dp_count, seq_count, seq_count, seq_count, seq_count, seq_count,
+                  group, group, seq_count),
+            compiler_params=pltpu.CompilerParams(collective_id=3, has_side_effects=True),
+            name="whole_step",
+        )(write_weight.T, decay_rows.T, scan_rows, back_rows, read_rows.T, input_rows)
+    else:
+        running = jnp.cumsum(decay_rows, axis=0)
+        overall = running[-1]
+        to_end = jnp.exp(overall[None, :] - running)
+        from_start = jnp.exp(running)
+        decay_total = jnp.exp(overall)
+
+        def widen(a):
+            return jnp.repeat(a, HEAD_DIM, axis=1)
+
+        scaled_scan = scan_rows.astype(f32) * widen(to_end)
+        scaled_back = back_rows.astype(f32) * widen(from_start)
+
+        def state_of(vectors, rows):
+            return lax.dot_general(
+                vectors.astype(f32), rows, (((0,), (0,)), ((), ())), precision=highest
+            ).astype(bf16)
+
+        reverse_local = state_of(read_rows, scaled_back)
+        decay_lanes = widen(decay_total[None]).reshape(seq_count, 1, width)
+        weight_half = write_weight.T.astype(bf16).reshape(2, state_size // 2, own_rows)
+        exchange = [
+            pltpu.VMEM((seq_count, state_size, width), bf16),
+            pltpu.VMEM((seq_count, state_size, width), bf16),
+        ]
+        piece = (state_size * own_rows // seq_count // 128, 128)
+        scan_split = scan_rows.reshape(length, heads, HEAD_DIM)
+        back_split = back_rows.reshape(length, heads, HEAD_DIM)
+        crossed = jnp.einsum("thp,shp->hts", scan_split, back_split, preferred_element_type=f32)
+        heads_running = running.T
+        spread = heads_running[:, None, :] - heads_running[:, :, None]
+        row_index = lax.broadcasted_iota(jnp.int32, (length, length), 0)
+        col_index = lax.broadcasted_iota(jnp.int32, (length, length), 1)
+        kernel_mat = (
+            jnp.where((row_index <= col_index)[None], jnp.exp(jnp.minimum(spread, 0.0)), 0.0) * crossed
+        )
+        weights, decays, grad_after = pl.pallas_call(
+            functools.partial(first_kernel, seq_count, dp_count),
+            out_shape=(
+                jax.ShapeDtypeStruct((dp_count,) + weight_half.shape, bf16),
+                jax.ShapeDtypeStruct(decay_lanes.shape, f32),
+                jax.ShapeDtypeStruct((state_size, channels), bf16),
+            ),
+            in_specs=[VMEM] * 3,
+            out_specs=[VMEM] * 3,
+            scratch_shapes=exchange + dma(dp_count, dp_count, seq_count, seq_count, seq_count),
+            compiler_params=pltpu.CompilerParams(collective_id=0, has_side_effects=True),
+            name="gather_reverse",
+        )(weight_half, reverse_local, decay_lanes)
+
+        weight_all = weights.reshape(dp_count, state_size, own_rows).transpose(1, 0, 2)
+        write_half = lax.dot_general(
+            input_rows, weight_all.reshape(state_size, model), (((1,), (1,)), ((), ())),
+            preferred_element_type=f32,
         ).astype(bf16)
-
-    reverse_local = state_of(read_rows, scaled_back)
-    decay_lanes = widen(decay_total[None]).reshape(seq_count, 1, width)
-    weight_half = write_weight.T.astype(bf16).reshape(2, state_size // 2, own_rows)
-    exchange = [
-        pltpu.VMEM((seq_count, state_size, width), bf16),
-        pltpu.VMEM((seq_count, state_size, width), bf16),
-    ]
-    weights, decays, grad_after = pl.pallas_call(
-        functools.partial(first_kernel, seq_count, dp_count),
-        out_shape=(
-            jax.ShapeDtypeStruct((dp_count,) + weight_half.shape, bf16),
-            jax.ShapeDtypeStruct(decay_lanes.shape, f32),
-            jax.ShapeDtypeStruct((state_size, channels), bf16),
-        ),
-        in_specs=[VMEM] * 3,
-        out_specs=[VMEM] * 3,
-        scratch_shapes=exchange + dma(dp_count, dp_count, seq_count, seq_count, seq_count),
-        compiler_params=pltpu.CompilerParams(collective_id=0, has_side_effects=True),
-        name="gather_reverse",
-    )(weight_half, reverse_local, decay_lanes)
-
-    weight_all = weights.reshape(dp_count, state_size, own_rows).transpose(1, 0, 2)
-    write_half = lax.dot_general(
-        input_rows, weight_all.reshape(state_size, model), (((1,), (1,)), ((), ())),
-        preferred_element_type=f32,
-    ).astype(bf16)
-    state_local = state_of(write_half, scaled_scan)
-    state_before = pl.pallas_call(
-        functools.partial(second_kernel, seq_count),
-        out_shape=jax.ShapeDtypeStruct((state_size, channels), bf16),
-        in_specs=[VMEM] * 2,
-        out_specs=VMEM,
-        scratch_shapes=exchange + dma(seq_count, seq_count),
-        compiler_params=pltpu.CompilerParams(collective_id=1, has_side_effects=True),
-        name="forward_states",
-    )(state_local, decays)
-
-    scan_split = scan_rows.reshape(length, heads, HEAD_DIM)
-    back_split = back_rows.reshape(length, heads, HEAD_DIM)
-    crossed = jnp.einsum("thp,shp->hts", scan_split, back_split, preferred_element_type=f32)
-    heads_running = running.T
-    spread = heads_running[:, None, :] - heads_running[:, :, None]
-    row_index = lax.broadcasted_iota(jnp.int32, (length, length), 0)
-    col_index = lax.broadcasted_iota(jnp.int32, (length, length), 1)
-    kernel_mat = (
-        jnp.where((row_index <= col_index)[None], jnp.exp(jnp.minimum(spread, 0.0)), 0.0) * crossed
-    )
-    kernel_sum = jnp.sum(kernel_mat, axis=0)
-    write_grad = jnp.dot(kernel_sum, read_rows.astype(f32), precision=highest)
-    write_grad = write_grad + lax.dot_general(
-        scaled_scan.astype(bf16), grad_after, (((1,), (1,)), ((), ())), preferred_element_type=f32
-    )
-    grad_half = write_grad.astype(bf16)
-    partial = lax.dot_general(
-        grad_half, input_rows, (((0,), (0,)), ((), ())), preferred_element_type=f32
-    ).astype(bf16)
-    chips = seq_count // 2
-    part = partial.reshape(state_size, dp_count, chips, 2, own_rows // seq_count)
-    piece = (state_size * own_rows // seq_count // 128, 128)
-    part = part.transpose(3, 2, 1, 0, 4).reshape((2, chips * dp_count) + piece)
-    grad_sum = pl.pallas_call(
-        functools.partial(third_kernel, seq_count, dp_count),
-        out_shape=jax.ShapeDtypeStruct((seq_count,) + piece, bf16),
-        in_specs=[VMEM],
-        out_specs=VMEM,
-        scratch_shapes=[pltpu.VMEM((chips * dp_count,) + piece, bf16)] * 3
-        + dma(chips * dp_count, chips * dp_count, seq_count),
-        compiler_params=pltpu.CompilerParams(collective_id=2, has_side_effects=True),
-        name="reduce_gradient",
-    )(part)
+        state_local = state_of(write_half, scaled_scan)
+        state_before = pl.pallas_call(
+            functools.partial(second_kernel, seq_count),
+            out_shape=jax.ShapeDtypeStruct((state_size, channels), bf16),
+            in_specs=[VMEM] * 2,
+            out_specs=VMEM,
+            scratch_shapes=exchange + dma(seq_count, seq_count),
+            compiler_params=pltpu.CompilerParams(collective_id=1, has_side_effects=True),
+            name="forward_states",
+        )(state_local, decays)
+
+        kernel_sum = jnp.sum(kernel_mat, axis=0)
+        write_grad = jnp.dot(kernel_sum, read_rows.astype(f32), precision=highest)
+        write_grad = write_grad + lax.dot_general(
+            scaled_scan.astype(bf16), grad_after, (((1,), (1,)), ((), ())), preferred_element_type=f32
+        )
+        grad_half = write_grad.astype(bf16)
+        partial = lax.dot_general(
+            grad_half, input_rows, (((0,), (0,)), ((), ())), preferred_element_type=f32
+        ).astype(bf16)
+        part = partial.reshape(state_size, dp_count, chips, 2, own_rows // seq_count)
+        part = part.transpose(3, 2, 1, 0, 4).reshape((2, chips * dp_count) + piece)
+        grad_sum = pl.pallas_call(
+            functools.partial(third_kernel, seq_count, dp_count),
+            out_shape=jax.ShapeDtypeStruct((seq_count,) + piece, bf16),
+            in_specs=[VMEM],
+            out_specs=VMEM,
+            scratch_shapes=[pltpu.VMEM((chips * dp_count,) + piece, bf16)] * 3
+            + dma(chips * dp_count, chips * dp_count, seq_count),
+            compiler_params=pltpu.CompilerParams(collective_id=2, has_side_effects=True),
+            name="reduce_gradient",
+        )(part)
+        def per_head(a):
+            return jnp.sum(a.reshape(a.shape[0], heads, HEAD_DIM), axis=2)
+
+        term_one = decay_total * jnp.sum(
+            per_head(grad_after.astype(f32) * state_before.astype(f32)), axis=0)
+        grad_write = jnp.dot(write_half, grad_after, preferred_element_type=f32)
+        second_rows = to_end * per_head(scan_rows.astype(f32) * grad_write)
+        term_two = jnp.cumsum(second_rows, axis=0) - second_rows
+        state_read = jnp.dot(read_rows, state_before, preferred_element_type=f32)
+        third_rows = from_start * per_head(back_rows.astype(f32) * state_read)
+        term_three = jnp.flip(jnp.cumsum(jnp.flip(third_rows, 0), axis=0), 0)
+        write_read = jnp.dot(write_half, read_rows.T, preferred_element_type=f32)
+        pairing = jnp.where((row_index < col_index)[None], kernel_mat * write_read[None], 0.0)
+        balance = (jnp.sum(pairing, axis=2) - jnp.sum(pairing, axis=1)).T
+        term_four = jnp.cumsum(balance, axis=0) - balance
+        decay_grad = term_one[None, :] + term_two + term_three + term_four
     grad_rows = grad_sum.reshape(seq_count, state_size, own_rows // seq_count).transpose(1, 0, 2)
     grad_rows = grad_rows.reshape(state_size, own_rows).astype(f32).T
     new_weight, new_first, new_second = adam_update(
         grad_rows, write_weight, first_moment, second_moment
     )
 
-    def per_head(a):
-        return jnp.sum(a.reshape(a.shape[0], heads, HEAD_DIM), axis=2)
-
-    term_one = decay_total * jnp.sum(
-        per_head(grad_after.astype(f32) * state_before.astype(f32)), axis=0)
-    grad_write = jnp.dot(write_half, grad_after, preferred_element_type=f32)
-    second_rows = to_end * per_head(scan_rows.astype(f32) * grad_write)
-    term_two = jnp.cumsum(second_rows, axis=0) - second_rows
-    state_read = jnp.dot(read_rows, state_before, preferred_element_type=f32)
-    third_rows = from_start * per_head(back_rows.astype(f32) * state_read)
-    term_three = jnp.flip(jnp.cumsum(jnp.flip(third_rows, 0), axis=0), 0)
-    write_read = jnp.dot(write_half, read_rows.T, preferred_element_type=f32)
-    pairing = jnp.where((row_index < col_index)[None], kernel_mat * write_read[None], 0.0)
-    balance = (jnp.sum(pairing, axis=2) - jnp.sum(pairing, axis=1)).T
-    term_four = jnp.cumsum(balance, axis=0) - balance
-    decay_grad = term_one[None, :] + term_two + term_three + term_four
     return (decay_grad[None], new_weight, new_first, new_second)
 
 

time: 94.5 us -> 53.8 us (0.57)
  Pallas kernels: 64.3 us -> 48.9 us
  local copies, waits for them, and re-layouts: 12.7 us -> 1.53 us
  matrix products: 9.9 us -> 0 us
  other arithmetic: 6.27 us -> 2.35 us
    pallas_call x3 -> x1, Pallas kernels: 64.3 us -> 48.9 us  [on_device(): pl.pallas_call(functools.partial(one_kernel, seq_count, dp_count), out_sh...]
    dot_general x9 -> x0, matrix products: 9.9 us -> none  [the longest x2 2.73 us: state_of(): lax.dot_general(vectors.astype(f32), rows, (((0,), (0,)), ((), ())), prec...]
    reshape x4 -> x0, local copies, waits for them, and re-layouts: 4.5 us -> none  [the longest x1 1.58 us: on_device(): weights.reshape(dp_count, state_size, own_rows).transpose(1, 0, 2)]
    broadcast_in_dim x3 -> x0, local copies, waits for them, and re-layouts: 1.84 us -> none  [widen(): return jnp.repeat(a, HEAD_DIM, axis=1)]
    reduce_sum x3 -> x0, other arithmetic: 1.53 us -> none  [the longest x1 1.32 us: per_head(): return jnp.sum(a.reshape(a.shape[0], heads, HEAD_DIM), axis=2)]
    another operation x4 -> x0, local copies, waits for them, and re-layouts: 1.49 us -> none  [the longest x1 0.7 us: on_device(): running = jnp.cumsum(decay_rows, axis=0)]
    squeeze x2 -> x0, local copies, waits for them, and re-layouts: 1.47 us -> none  [the longest x1 0.95 us: on_device(): decay_rows = log_decay[0]]
    mul x2 -> x0, local copies, waits for them, and re-layouts: 1.43 us -> none  [on_device(): second_rows = to_end * per_head(scan_rows.astype(f32) * grad_write)]
where the time goes in v2:
time: 53.8 us; the launch traced here: 53.5 us
  Pallas kernels  48.9 us (91%)
  other arithmetic  2.35 us (4%)
  local copies, waits for them, and re-layouts  1.53 us (3%)
  between operations  0.67 us (1%)
    pallas_call x1, Pallas kernels, on_device(): pl.pallas_call(functools.partial(one_kernel, seq_count, dp_count), out_sh...  48.9 us
    sub x1, other arithmetic, adam_update(): weight_rows - learn_rate * (first_hat / (jnp.sqrt(second_hat) + epsilon)...  2.35 us
    unnamed x7, local copies, waits for them, and re-layouts  1.53 us

profile of v2, /device:TPU:0, one launch (start us, length us, event | category | flops | bytes accessed | tf_op | source)
XLA Modules:
  0.0 53.5 jit_solution(7139782698249565478)
XLA Ops:
  0.6 0.0 copy-start
  0.6 0.0 copy-start.1
  0.7 0.0 copy-start.2
  0.7 48.9 %whole_step.1 = (f32[128,32]{1,0:T(8,128)}, bf16[16,64,128]{2,1,0:T(8,128)(2,1)}) custom-call(f32[64,2048]{1,0:T(8,128)} %bitcast.35, f32[32,128]{1,0:T(8,128)} %bitcast.40, bf16[128,2048]{1,0:T(8,128)(2,1)} %bitcast.37, bf16[128,2048]{1,0:T(8,128)(2,1)} %bitcast.38, bf16[64,128]{1,0:T(8,128)(2,1)} %bitcast.41, bf16[128,4096]{1,0:T(8,128)(2,1)} %bitcast.36), custom_call_target="tpu_custom_call" | custom-call | tf_op jit(solution)/shard_map/whole_step/pallas_call | solution.py:502
  49.6 1.5 %copy.14 = f32[1,128,32]{1,2,0:T(8,128)} copy(f32[1,128,32]{2,1,0:T(8,128)} %bitcast.39) | data formatting | bytes 32768
  51.1 0.0 copy-done
  51.1 0.0 copy-done.1
  51.1 0.0 copy-done.2
  51.1 2.4 %multiply_subtract_fusion = (f32[2048,64]{0,1:T(8,128)}, f32[2048,64]{0,1:T(8,128)}, f32[2048,64]{0,1:T(8,128)}) fusion(f32[2048,64]{0,1:T(8,128)S(1)} %copy-done, f32[2048,64]{0,1:T(8,128)S(1)} %copy-done.1, f32[2048,64]{0,1:T(8,128)S(1)} %copy-done.2, bf16[16,64,128]{2,1,0:T(8,128)(2,1)} %get-tuple-element.7), kind=kLoop, calls=%fused_computation.6 | loop fusion | flops 2097152 | bytes 3407872 | tf_op jit(solution)/shard_map/sub | solution.py:466
Async XLA Ops:
  0.6 50.5 %copy-start = (f32[2048,64]{0,1:T(8,128)S(1)}, f32[2048,64]{0,1:T(8,128)}, u32[]{:S(2)}) copy-start(f32[2048,64]{0,1:T(8,128)} %param.13) | copy-start | bytes 1572868
  0.6 50.5 %copy-start.1 = (f32[2048,64]{0,1:T(8,128)S(1)}, f32[2048,64]{0,1:T(8,128)}, u32[]{:S(2)}) copy-start(f32[2048,64]{0,1:T(8,128)} %param.14) | copy-start | bytes 1572868
  0.7 50.5 %copy-start.2 = (f32[2048,64]{0,1:T(8,128)S(1)}, f32[2048,64]{0,1:T(8,128)}, u32[]{:S(2)}) copy-start(f32[2048,64]{0,1:T(8,128)} %param.15) | copy-start | bytes 1572868

commit v3 on v2

--- a/solution.py
+++ b/solution.py
@@ -67,7 +67,7 @@
             def _():
                 self.outward(i, i).wait_recv()
 
-            self.sent[i] = running.astype(bf16)
+            self.sent[i] = running.astype(self.sent.dtype)
             new = self.decay[i] * running + self.gathered[i].astype(f32)
 
             @pl.when(i != me)
@@ -250,7 +250,8 @@
                row_sums, col_sums, weights, decays, forward_local, reverse_got, reverse_sent, forward_got,
                forward_sent, part, halves, summed, pieces,
                w_send, w_recv, p_send, p_recv, d_send, d_recv, a_send, a_recv, b_send, b_recv,
-               e_send, e_recv, f_send, f_recv, h_send, h_recv, s_send, s_recv, g_send, g_recv):
+               e_send, e_recv, f_send, f_recv, h_send, h_recv, s_send, s_recv, g_send, g_recv,
+               r_send, r_recv):
     seq_me, dp_me = lax.axis_index("seq"), lax.axis_index("dp")
     core = lax.rem(seq_me, 2)
     chip = seq_me // 2
@@ -322,6 +323,13 @@
         return remote(total.at[seq_me], total.at[source], g_send.at[j], g_recv.at[source],
                       {"seq": j})
 
+    def relay(j, source):
+        return remote(total.at[j], total.at[source], r_send.at[j], r_recv.at[source],
+                      {"seq": partner})
+
+    def fellow(k):
+        return lax.rem(seq_me + 2 * k, seq_count)
+
     loop(1, dp_count, lambda k: across(lax.rem(dp_me + k, dp_count), dp_me).start())
     loop(1, seq_count, lambda k: tell(lax.rem(seq_me + k, seq_count), seq_me).start())
     reverse = Scan(seq_count, seq_me, reverse_local, decays, reverse_got, reverse_sent, grad_after,
@@ -376,7 +384,7 @@
         forward_local[:, low : low + step] = (
             jnp.dot(write, scan_high, preferred_element_type=f32)
             + jnp.dot(write, scan_low, preferred_element_type=f32)
-        ).astype(bf16)
+        )
     forward.start()
 
     reverse.arrive()
@@ -392,8 +400,6 @@
         part[0, g] = term[:, :wide]
         part[1, g] = term[:, wide:]
     loop(1, group + 1, lambda k: half(lax.rem(mine + k, group)).start())
-    forward.combine(False)
-
     def pair(k):
         g = lax.rem(mine + k, group)
         half(g).wait_recv()
@@ -404,6 +410,7 @@
             scatter(g, mine).start()
 
     loop(1, group + 1, pair)
+    forward.combine(False)
 
     read_turned = read_rows[...].astype(f32).T.astype(bf16)
     write_read = jnp.where(row_index < col_index, nt(write_rows, read_turned), 0.0)
@@ -421,25 +428,38 @@
 
     own = part[core, mine].astype(f32) + halves[mine].astype(f32)
     total[seq_me] = lax.fori_loop(1, group, collect, own).astype(bf16)
-    loop(1, seq_count, lambda k: share(lax.rem(seq_me + k, seq_count), seq_me).start())
+    loop(1, seq_count // 2, lambda k: share(fellow(k), seq_me).start())
+    relay(seq_me, seq_me).start()
     forward.arrive()
-    state_read = jnp.dot(read_turned, state_before[...], preferred_element_type=f32)
+    state_high, state_low = split(state_before[...])
+    state_read = (jnp.dot(read_turned, state_high, preferred_element_type=f32)
+                  + jnp.dot(read_turned, state_low, preferred_element_type=f32))
     third = from_start * per_head(back_rows[...].astype(f32) * state_read)
-    both = jnp.sum(grad_after[...].astype(f32) * state_before[...].astype(f32), axis=0,
+    both = jnp.sum(grad_after[...].astype(f32) * state_before[...], axis=0,
                    keepdims=True)
     first = jnp.exp(overall) * per_head(jnp.broadcast_to(both, (8, channels)))[:1]
-    decay_grad[...] = (
+    decay_grad[...] = jnp.transpose(
         first
         + jnp.dot(before, second, precision=highest)
         - exact(before, col_sums[...])
         + jnp.dot(onward, third, precision=highest)
     )
 
+    def shared(k):
+        j = fellow(seq_count // 2 - k)
+        share(j, j).wait_recv()
+        relay(j, j).start()
+
+    loop(1, seq_count // 2, shared)
+
     def end(k):
-        j = lax.rem(seq_me + seq_count - k, seq_count)
-        share(j, j).wait_recv()
-        share(j, j).wait_send()
-        tell(j, j).wait_send()
+        share(fellow(k), seq_me).wait_send()
+
+    def relayed(k):
+        j = fellow(k)
+        relay(j, j).wait_send()
+        other = j + 1 - 2 * core
+        relay(other, other).wait_recv()
 
     def dp_end(k):
         d = lax.rem(dp_me + k, dp_count)
@@ -451,7 +471,9 @@
     forward.drain()
     loop(1, group + 1, lambda k: half(lax.rem(mine + k, group)).wait_send())
     loop(1, group, lambda k: scatter(lax.rem(mine + k, group), 0).wait_send())
-    loop(1, seq_count, end)
+    loop(1, seq_count, lambda k: tell(lax.rem(seq_me + k, seq_count), seq_me).wait_send())
+    loop(1, seq_count // 2, end)
+    loop(0, seq_count // 2, relayed)
 
 
 def dma(*sizes):
@@ -497,19 +519,21 @@
     if own_rows % (128 * seq_count) == 0:
         piece = (state_size, own_rows // seq_count)
         exchange = [pltpu.VMEM((seq_count, state_size, width), bf16)] * 2
+        exact_exchange = [pltpu.VMEM((seq_count, state_size, width), f32)] * 2
         states = pltpu.VMEM((state_size, channels), bf16)
+        exact_states = pltpu.VMEM((state_size, channels), f32)
         halves = (2, state_size // 2, own_rows)
         decay_grad, grad_sum = pl.pallas_call(
             functools.partial(one_kernel, seq_count, dp_count),
             out_shape=(
-                jax.ShapeDtypeStruct((length, heads), f32),
+                jax.ShapeDtypeStruct((heads, length), f32),
                 jax.ShapeDtypeStruct((seq_count,) + piece, bf16),
             ),
             in_specs=[VMEM] * 6,
             out_specs=[VMEM] * 2,
             scratch_shapes=[
                 states,
-                states,
+                exact_states,
                 pltpu.VMEM(halves, bf16),
                 states,
                 pltpu.VMEM((seq_count, 1, width), f32),
@@ -519,17 +543,18 @@
                 pltpu.VMEM((heads, length), f32),
                 pltpu.VMEM((dp_count,) + halves, bf16),
                 pltpu.VMEM((seq_count, 1, width), f32),
-                states,
+                exact_states,
             ]
             + exchange
-            + exchange
+            + exact_exchange
             + [pltpu.VMEM((2, group) + piece, bf16)]
             + [pltpu.VMEM((group,) + piece, bf16)] * 3
             + dma(dp_count, dp_count, seq_count, seq_count, seq_count, seq_count, seq_count,
-                  group, group, seq_count),
+                  group, group, seq_count, seq_count),
             compiler_params=pltpu.CompilerParams(collective_id=3, has_side_effects=True),
             name="whole_step",
         )(write_weight.T, decay_rows.T, scan_rows, back_rows, read_rows.T, input_rows)
+        decay_grad = decay_grad.T
     else:
         running = jnp.cumsum(decay_rows, axis=0)
         overall = running[-1]
@@ -546,9 +571,9 @@
         def state_of(vectors, rows):
             return lax.dot_general(
                 vectors.astype(f32), rows, (((0,), (0,)), ((), ())), precision=highest
-            ).astype(bf16)
-
-        reverse_local = state_of(read_rows, scaled_back)
+            )
+
+        reverse_local = state_of(read_rows, scaled_back).astype(bf16)
         decay_lanes = widen(decay_total[None]).reshape(seq_count, 1, width)
         weight_half = write_weight.T.astype(bf16).reshape(2, state_size // 2, own_rows)
         exchange = [
@@ -588,10 +613,10 @@
         state_local = state_of(write_half, scaled_scan)
         state_before = pl.pallas_call(
             functools.partial(second_kernel, seq_count),
-            out_shape=jax.ShapeDtypeStruct((state_size, channels), bf16),
+            out_shape=jax.ShapeDtypeStruct((state_size, channels), f32),
             in_specs=[VMEM] * 2,
             out_specs=VMEM,
-            scratch_shapes=exchange + dma(seq_count, seq_count),
+            scratch_shapes=[pltpu.VMEM((seq_count, state_size, width), f32)] * 2 + dma(seq_count, seq_count),
             compiler_params=pltpu.CompilerParams(collective_id=1, has_side_effects=True),
             name="forward_states",
         )(state_local, decays)
@@ -625,7 +650,7 @@
         grad_write = jnp.dot(write_half, grad_after, preferred_element_type=f32)
         second_rows = to_end * per_head(scan_rows.astype(f32) * grad_write)
         term_two = jnp.cumsum(second_rows, axis=0) - second_rows
-        state_read = jnp.dot(read_rows, state_before, preferred_element_type=f32)
+        state_read = jnp.dot(read_rows.astype(f32), state_before, precision=highest)
         third_rows = from_start * per_head(back_rows.astype(f32) * state_read)
         term_three = jnp.flip(jnp.cumsum(jnp.flip(third_rows, 0), axis=0), 0)
         write_read = jnp.dot(write_half, read_rows.T, preferred_element_type=f32)

time: 53.8 us -> 60.7 us (1.13)
  Pallas kernels: 48.9 us -> 56.9 us
  local copies, waits for them, and re-layouts: 1.53 us -> 0.62 us
    pallas_call x1, Pallas kernels: 48.9 us -> 56.9 us  [on_device(): pl.pallas_call(functools.partial(one_kernel, seq_count, dp_count), out_sh...]
    unnamed x7 -> x9, local copies, waits for them, and re-layouts: 1.53 us -> 0.62 us
where the time goes in v3:
time: 60.7 us; the launch traced here: 60.6 us
  Pallas kernels  56.9 us (94%)
  other arithmetic  2.35 us (4%)
  between operations  0.7 us (1%)
  local copies, waits for them, and re-layouts  0.62 us (1%)
    pallas_call x1, Pallas kernels, on_device(): pl.pallas_call(functools.partial(one_kernel, seq_count, dp_count), out_sh...  56.9 us
    sub x1, other arithmetic, adam_update(): weight_rows - learn_rate * (first_hat / (jnp.sqrt(second_hat) + epsilon)...  2.35 us

profile of v3, /device:TPU:0, one launch (start us, length us, event | category | flops | bytes accessed | tf_op | source)
XLA Modules:
  0.0 60.6 jit_solution(5731636708774377630)
XLA Ops:
  0.6 0.0 copy-start
  0.6 0.0 copy-start.1
  0.7 0.0 copy-start.2
  0.7 56.9 %whole_step.1 = (f32[32,128]{1,0:T(8,128)}, bf16[16,64,128]{2,1,0:T(8,128)(2,1)}) custom-call(f32[64,2048]{1,0:T(8,128)} %bitcast.37, f32[32,128]{1,0:T(8,128)} %bitcast.42, bf16[128,2048]{1,0:T(8,128)(2,1)} %bitcast.39, bf16[128,2048]{1,0:T(8,128)(2,1)} %bitcast.40, bf16[64,128]{1,0:T(8,128)(2,1)} %bitcast.43, bf16[128,4096]{1,0:T(8,128)(2,1)} %bitcast.38), custom_call_target="tpu_custom_call" | custom-call | tf_op jit(solution)/shard_map/whole_step/pallas_call | solution.py:526
  57.6 0.0 copy-done
  57.6 0.0 copy-done.1
  57.6 0.0 copy-done.2
  57.6 0.0 copy-start.3
  57.6 2.4 %multiply_subtract_fusion = (f32[2048,64]{0,1:T(8,128)}, f32[2048,64]{0,1:T(8,128)}, f32[2048,64]{0,1:T(8,128)}) fusion(f32[2048,64]{0,1:T(8,128)S(1)} %copy-done, f32[2048,64]{0,1:T(8,128)S(1)} %copy-done.1, f32[2048,64]{0,1:T(8,128)S(1)} %copy-done.2, bf16[16,64,128]{2,1,0:T(8,128)(2,1)} %get-tuple-element.7), kind=kLoop, calls=%fused_computation.6 | loop fusion | flops 2097152 | bytes 3407872 | tf_op jit(solution)/shard_map/sub | solution.py:488
  60.0 0.0 copy-done.3
  60.0 0.6 copy.19
Async XLA Ops:
  0.6 57.0 %copy-start = (f32[2048,64]{0,1:T(8,128)S(1)}, f32[2048,64]{0,1:T(8,128)}, u32[]{:S(2)}) copy-start(f32[2048,64]{0,1:T(8,128)} %param.13) | copy-start | bytes 1572868
  0.6 57.0 %copy-start.1 = (f32[2048,64]{0,1:T(8,128)S(1)}, f32[2048,64]{0,1:T(8,128)}, u32[]{:S(2)}) copy-start(f32[2048,64]{0,1:T(8,128)} %param.14) | copy-start | bytes 1572868
  0.7 57.0 %copy-start.2 = (f32[2048,64]{0,1:T(8,128)S(1)}, f32[2048,64]{0,1:T(8,128)}, u32[]{:S(2)}) copy-start(f32[2048,64]{0,1:T(8,128)} %param.15) | copy-start | bytes 1572868
  57.6 2.4 %copy-start.3 = (f32[32,128]{1,0:T(8,128)S(1)}, f32[32,128]{1,0:T(8,128)}, u32[]{:S(2)}) copy-start(f32[32,128]{1,0:T(8,128)} %get-tuple-element.6) | copy-start | bytes 49156

commit v4 on v3

--- a/solution.py
+++ b/solution.py
@@ -384,7 +384,7 @@
         forward_local[:, low : low + step] = (
             jnp.dot(write, scan_high, preferred_element_type=f32)
             + jnp.dot(write, scan_low, preferred_element_type=f32)
-        )
+        ).astype(bf16)
     forward.start()
 
     reverse.arrive()
@@ -519,7 +519,7 @@
     if own_rows % (128 * seq_count) == 0:
         piece = (state_size, own_rows // seq_count)
         exchange = [pltpu.VMEM((seq_count, state_size, width), bf16)] * 2
-        exact_exchange = [pltpu.VMEM((seq_count, state_size, width), f32)] * 2
+        exact_exchange = [pltpu.VMEM((seq_count, state_size, width), d) for d in (bf16, f32)]
         states = pltpu.VMEM((state_size, channels), bf16)
         exact_states = pltpu.VMEM((state_size, channels), f32)
         halves = (2, state_size // 2, own_rows)
@@ -543,7 +543,7 @@
                 pltpu.VMEM((heads, length), f32),
                 pltpu.VMEM((dp_count,) + halves, bf16),
                 pltpu.VMEM((seq_count, 1, width), f32),
-                exact_states,
+                states,
             ]
             + exchange
             + exact_exchange

time: 60.7 us -> 55.6 us (0.916)
  Pallas kernels: 56.9 us -> 51.8 us
    pallas_call x1, Pallas kernels: 56.9 us -> 51.8 us  [on_device(): pl.pallas_call(functools.partial(one_kernel, seq_count, dp_count), out_sh...]
where the time goes in v4:
time: 55.6 us; the launch traced here: 55.5 us
  Pallas kernels  51.8 us (93%)
  other arithmetic  2.35 us (4%)
  between operations  0.7 us (1%)
  local copies, waits for them, and re-layouts  0.62 us (1%)
    pallas_call x1, Pallas kernels, on_device(): pl.pallas_call(functools.partial(one_kernel, seq_count, dp_count), out_sh...  51.8 us
    sub x1, other arithmetic, adam_update(): weight_rows - learn_rate * (first_hat / (jnp.sqrt(second_hat) + epsilon)...  2.35 us

profile of v4, /device:TPU:0, one launch (start us, length us, event | category | flops | bytes accessed | tf_op | source)
XLA Modules:
  0.0 55.5 jit_solution(12639845146789300200)
XLA Ops:
  0.6 0.0 copy-start
  0.6 0.0 copy-start.1
  0.7 0.0 copy-start.2
  0.7 51.8 %whole_step.1 = (f32[32,128]{1,0:T(8,128)}, bf16[16,64,128]{2,1,0:T(8,128)(2,1)}) custom-call(f32[64,2048]{1,0:T(8,128)} %bitcast.37, f32[32,128]{1,0:T(8,128)} %bitcast.42, bf16[128,2048]{1,0:T(8,128)(2,1)} %bitcast.39, bf16[128,2048]{1,0:T(8,128)(2,1)} %bitcast.40, bf16[64,128]{1,0:T(8,128)(2,1)} %bitcast.43, bf16[128,4096]{1,0:T(8,128)(2,1)} %bitcast.38), custom_call_target="tpu_custom_call" | custom-call | tf_op jit(solution)/shard_map/whole_step/pallas_call | solution.py:526
  52.5 0.0 copy-done
  52.5 0.0 copy-done.1
  52.5 0.0 copy-done.2
  52.5 0.0 copy-start.3
  52.5 2.4 %multiply_subtract_fusion = (f32[2048,64]{0,1:T(8,128)}, f32[2048,64]{0,1:T(8,128)}, f32[2048,64]{0,1:T(8,128)}) fusion(f32[2048,64]{0,1:T(8,128)S(1)} %copy-done, f32[2048,64]{0,1:T(8,128)S(1)} %copy-done.1, f32[2048,64]{0,1:T(8,128)S(1)} %copy-done.2, bf16[16,64,128]{2,1,0:T(8,128)(2,1)} %get-tuple-element.7), kind=kLoop, calls=%fused_computation.6 | loop fusion | flops 2097152 | bytes 3407872 | tf_op jit(solution)/shard_map/sub | solution.py:488
  54.8 0.0 copy-done.3
  54.9 0.6 %copy.19 = f32[1,128,32]{1,2,0:T(8,128)} copy(f32[1,128,32]{1,2,0:T(8,128)S(1)} %bitcast.41) | data formatting | bytes 32768
Async XLA Ops:
  0.6 51.8 %copy-start = (f32[2048,64]{0,1:T(8,128)S(1)}, f32[2048,64]{0,1:T(8,128)}, u32[]{:S(2)}) copy-start(f32[2048,64]{0,1:T(8,128)} %param.13) | copy-start | bytes 1572868
  0.6 51.8 %copy-start.1 = (f32[2048,64]{0,1:T(8,128)S(1)}, f32[2048,64]{0,1:T(8,128)}, u32[]{:S(2)}) copy-start(f32[2048,64]{0,1:T(8,128)} %param.14) | copy-start | bytes 1572868
  0.7 51.8 %copy-start.2 = (f32[2048,64]{0,1:T(8,128)S(1)}, f32[2048,64]{0,1:T(8,128)}, u32[]{:S(2)}) copy-start(f32[2048,64]{0,1:T(8,128)} %param.15) | copy-start | bytes 1572868
  52.5 2.4 %copy-start.3 = (f32[32,128]{1,0:T(8,128)S(1)}, f32[32,128]{1,0:T(8,128)}, u32[]{:S(2)}) copy-start(f32[32,128]{1,0:T(8,128)} %get-tuple-element.6) | copy-start | bytes 49156
